TPU v7x, 512 devices: a whole 4x4x16 slice. The times are simulated.
512 devices in a mesh: pipe: 8 (over y_lo, x), dp: 64 (over z, y_hi, core).
Axes of the slice: x: 4, y: 4 (y_hi: 2, y_lo: 2; y = y_hi * 2 + y_lo), z: 16, core: 2. Of those that a mesh axis runs over, the one named last changes fastest.
Arguments:
- visual_fragments: bfloat16 [8, 64, 64, 1152], P(None, 'dp'), may hold values from -6 to 6
- widening_kernel: bfloat16 [8, 1152, 2176], P('pipe', None, 'dp'), may hold values from -0.1875 to 0.1875
- narrowing_kernel: bfloat16 [8, 2176, 1152], P('pipe', 'dp'), may hold values from -0.125 to 0.125
- caption_outputs: bfloat16 [4608, 1152], P(('pipe', 'dp')), may hold values from -6 to 6
- earlier_averaged: float32 [4096, 1152], P(('pipe', 'dp')), may hold values from -6 to 6
- match_targets: int32 [4608], replicated, may hold values from 0 to 4607, each once
- score_scaling: float32 [1], replicated, may hold values from 5 to 15
- score_shift: float32 [1], replicated, may hold values from -4 to -2
Outputs:
- image_grad: float32 [4608, 1152], P(('pipe', 'dp'))
- text_grad: float32 [4608, 1152], P(('pipe', 'dp'))
Inputs may be any that keep to these rules, and one draw needn't show every extreme that they name: match_targets is a permutation: every text is the positive of exactly one image.
All inputs are finite; a program needn't handle non-finite values.
Results may differ from a plain program's by a relative error of at most 0.017.
Values may be sent and summed in bfloat16 or wider, within the bound.
No kernel may reach another device: no remote copies, remote signals or barrier semaphores. Data moves between devices by JAX's collectives and lax.ppermute only.
A program may use at most 128 MiB of HBM per device.

v0:
```python
import jax
import jax.numpy as jnp
from jax import lax
from jax.sharding import PartitionSpec as P


def from_behind(value, axis, steps):
    count = lax.axis_size(axis)
    pairs = [(source, (source + steps) % count) for source in range(count)]
    return lax.ppermute(value, axis, pairs)


def layer_norm(hidden_rows):
    values = hidden_rows.astype(jnp.float32)
    centre = jnp.mean(values, axis=-1, keepdims=True)
    shifted = values - centre
    variance = jnp.mean(shifted * shifted, axis=-1, keepdims=True)
    return (shifted * lax.rsqrt(variance + 1e-06)).astype(jnp.bfloat16)


def section_block(hidden_rows, w_up, w_down):
    normed = layer_norm(hidden_rows)
    pre_act = jnp.dot(normed, w_up, preferred_element_type=jnp.float32)
    activated = jax.nn.gelu(pre_act, approximate=True).astype(jnp.bfloat16)
    updated = hidden_rows.astype(jnp.float32) + jnp.dot(
        activated, w_down, preferred_element_type=jnp.float32
    )
    return updated.astype(jnp.bfloat16)


def unit_rows(values):
    values = values.astype(jnp.float32)
    total = jnp.sum(values * values, axis=-1, keepdims=True)
    return (values * lax.rsqrt(total + 1e-06)).astype(jnp.bfloat16)


def coupling_factors(
    picture_group, source_caption_tile, match_entries, target_tile, sharpness_factor, shift_addend
):
    similarity_scores = (
        sharpness_factor
        * jnp.dot(picture_group, source_caption_tile.T, preferred_element_type=jnp.float32)
        + shift_addend
    )
    matching_couples = match_entries[:, None] == target_tile[None, :]
    coefficient_grid = jnp.where(
        matching_couples,
        -sharpness_factor * jax.nn.sigmoid(-similarity_scores),
        sharpness_factor * jax.nn.sigmoid(similarity_scores),
    )
    return coefficient_grid.astype(jnp.bfloat16)


def body(
    visual_fragments,
    widening_kernel,
    narrowing_kernel,
    caption_outputs,
    earlier_averaged,
    match_targets,
    score_scaling,
    score_shift,
):
    sections = lax.axis_size("pipe")
    section_id = lax.axis_index("pipe")
    data_count = lax.axis_size("dp")
    data_id = lax.axis_index("dp")
    micros, img_mb, patch_count, model_width = visual_fragments.shape
    tok_rows = img_mb * patch_count
    sharpness_factor = score_scaling[0]
    shift_addend = score_shift[0]
    caption_vectors = unit_rows(caption_outputs)
    up_full, down_full = (
        lax.all_gather(widening_kernel, "dp", axis=2, tiled=True),
        lax.all_gather(narrowing_kernel, "dp", axis=1, tiled=True),
    )
    up_full = up_full[0]
    down_full = down_full[0]
    panels = visual_fragments.reshape(micros, tok_rows, model_width)

    def advance(step, current):
        pick = jnp.clip(sections - 1 - step, 0, micros - 1)
        incoming = lax.dynamic_index_in_dim(panels, pick, 0, keepdims=False)
        current = jnp.where((section_id == 0) & (step < sections), incoming, current)
        active = (step >= section_id) & (step - section_id < sections)
        current = lax.cond(
            active,
            lambda carried: section_block(carried, up_full, down_full),
            lambda carried: carried,
            current,
        )
        return from_behind(current, "pipe", 1)

    finished = lax.fori_loop(
        0, 2 * sections - 1, advance, jnp.zeros((tok_rows, model_width), jnp.bfloat16)
    )
    pooled = jnp.mean(
        finished.astype(jnp.float32).reshape(img_mb, patch_count, model_width), axis=1
    )
    picture_vectors = jnp.concatenate([unit_rows(pooled), unit_rows(earlier_averaged)], axis=0)
    rows_dev = picture_vectors.shape[0]
    row_width = data_count * rows_dev
    text_row_block = lax.all_gather(caption_vectors, "dp", axis=0, tiled=True)
    image_column_block = lax.all_gather(picture_vectors, "pipe", axis=0, tiled=True)
    label_table = match_targets.reshape(sections, row_width)
    label_columns = lax.dynamic_slice_in_dim(label_table, data_id * rows_dev, rows_dev, 1).reshape(
        -1
    )
    column_text_block = section_id * row_width + jnp.arange(row_width, dtype=jnp.int32)
    grid_weights = coupling_factors(
        image_column_block,
        text_row_block,
        label_columns,
        column_text_block,
        sharpness_factor,
        shift_addend,
    )
    block = grid_weights
    image_grad = lax.psum_scatter(
        jnp.dot(block, text_row_block, preferred_element_type=jnp.float32).astype(jnp.bfloat16),
        "pipe",
        scatter_dimension=0,
        tiled=True,
    ).astype(jnp.float32)
    block = grid_weights
    text_grad = lax.psum_scatter(
        jnp.dot(block.T, image_column_block, preferred_element_type=jnp.float32),
        "dp",
        scatter_dimension=0,
        tiled=True,
    )
    return (image_grad, text_grad)


def solution(mesh):
    placed = (
        P(None, "dp", None, None),
        P("pipe", None, "dp"),
        P("pipe", "dp", None),
        P(("pipe", "dp"), None),
        P(("pipe", "dp"), None),
        P(),
        P(),
        P(),
    )
    return jax.shard_map(
        body,
        mesh=mesh,
        in_specs=placed,
        out_specs=(P(("pipe", "dp"), None), P(("pipe", "dp"), None)),
        check_vma=False,
    )
```

profile of v0, /device:TPU:1, one launch (start us, length us, event | category | flops | bytes accessed | tf_op | source)
XLA Modules:
  0.0 1396.2 jit_solution(13821860944951176592)
XLA Ops:
  17.2 145.3 %all-gather.10.cloned.1.call-done = bf16[64,9,1152]{2,1,0:T(8,128)(2,1)} async-done(((bf16[1,9,1152]{2,1,0:T(8,128)(2,1)}), bf16[64,9,1152]{2,1,0:T(8,128)(2,1)}) %all-gather.10.cloned.1.call-update) | async-done | bytes 1327120 | tf_op jit(solution)/shard_map/all_gather | solution.py:103
  165.1 165.6 %all-gather.8.cloned.1.call-done = bf16[1,2176,1152]{2,0,1:T(2,128)(2,1)} async-done(((bf16[1,34,1152]{2,0,1:T(2,128)(2,1)}), bf16[1,2176,1152]{2,0,1:T(2,128)(2,1)}) %all-gather.8.cloned.1.call-update) | async-done | bytes 5013520 | tf_op jit(solution)/shard_map/all_gather | solution.py:75
  330.7 6.9 copy.20
  337.6 161.9 %all-gather.6.cloned.1.call-done = bf16[1,1152,2176]{1,0,2:T(2,128)(2,1)} async-done(((bf16[1,1152,34]{1,0,2:T(2,128)(2,1)}), bf16[1,1152,2176]{1,0,2:T(2,128)(2,1)}) %all-gather.6.cloned.1.call-update) | async-done | bytes 5013520 | tf_op jit(solution)/shard_map/all_gather | solution.py:74
  499.5 22.0 %copy.16 = bf16[1,1152,2176]{2,1,0:T(8,128)(2,1)} copy(bf16[1,1152,2176]{1,0,2:T(2,128)(2,1)} %all-gather.6.cloned.1.call-done) | data formatting | bytes 10027008 | tf_op jit(solution)/shard_map/all_gather | solution.py:74
  521.5 213.1 %while.14 = (s32[]{:T(128)}, bf16[64,1152]{1,0:T(8,128)(2,1)S(1)}, s32[]{:T(128)}, pred[]{:T(512)}, bf16[8,64,1152]{2,1,0:T(8,128)(2,1)}, /*index=5*/bf16[1152,2...) while((s32[]{:T(128)}, bf16[64,1152]{1,0:T(8,128)(2,1)S(1)}, ...), condition=%wide.region_5.6_spmd, body=%wide.region_0.5_spmd.sunk | while | flops 644014144 | bytes 11946512 | solution.py:94
  522.5 6.1 conditional.2
  530.5 7.3 collective-permute-done
  538.7 6.1 conditional.2
  553.7 6.1 conditional.2
  568.7 6.1 conditional.2
  583.7 6.1 conditional.2
  598.8 6.1 conditional.2
  613.8 6.1 conditional.2
  628.8 6.1 conditional.2
  656.8 10.0 collective-permute-done
  669.7 10.0 collective-permute-done
  682.6 10.0 collective-permute-done
  695.5 11.4 collective-permute-done
  709.9 11.8 collective-permute-done
  724.5 10.1 collective-permute-done
  736.0 22.1 %all-gather = bf16[8,9,1152]{2,1,0:T(8,128)(2,1)S(1)} all-gather(bf16[1,9,1152]{2,1,0:T(8,128)(2,1)S(1)} %maximum_bitcast_fusion), channel_id=1, replica_groups=mesh['pipe'=8,'dp'=64] {'pipe'}, dimensions={0}, use_global_device_ids=true | all-gather | bytes 186624 | tf_op jit(solution)/shard_map/all_gather | solution.py:104
  765.9 91.5 %all-reduce.5.cloned.1.call-done = bf16[72,1152]{1,0:T(8,128)(2,1)} async-done(((bf16[72,1152]{1,0:T(8,128)(2,1)}), bf16[72,1152]{1,0:T(8,128)(2,1)}) %all-reduce.5.cloned.1.call-update) | async-done | bytes 165904
  858.8 529.3 %all-reduce.7.cloned.1.call-done = f32[576,1152]{1,0:T(8,128)} async-done(((f32[576,1152]{1,0:T(8,128)}), f32[576,1152]{1,0:T(8,128)}) %all-reduce.7.cloned.1.call-update) | async-done | bytes 2654224
  (130 shorter events, 163.3 us)
Async XLA Ops:
  7.2 155.3 %all-gather.10.cloned.1.call-start = ((), (), s32[]{:S(2)}) async-start(), calls=%async_computation.2 | async-start | bytes 2396160 | tf_op jit(solution)/shard_map/all_gather | solution.py:103
  9.6 321.1 %all-gather.8.cloned.1.call-start = ((), (), s32[]{:S(2)}) async-start(), calls=%async_computation.1 | async-start | bytes 10183680 | tf_op jit(solution)/shard_map/all_gather | solution.py:75
  11.4 488.1 %all-gather.6.cloned.1.call-start = ((), (), s32[]{:S(2)}) async-start(), calls=%async_computation | async-start | bytes 10183680 | tf_op jit(solution)/shard_map/all_gather | solution.py:74
  13.1 844.3 %all-reduce.5.cloned.1.call-start = ((), (), s32[]{:S(2)}) async-start(), calls=%async_computation.3 | async-start | bytes 331776
  528.6 9.2 collective-permute-start
  544.8 8.0 collective-permute-start
  559.8 8.0 collective-permute-start
  574.8 8.0 collective-permute-start
  589.8 8.0 collective-permute-start
  604.9 8.0 collective-permute-start
  619.9 8.0 collective-permute-start
  634.9 8.0 collective-permute-start
  643.8 10.1 collective-permute-start
  654.9 12.0 collective-permute-start
  667.8 12.0 collective-permute-start
  680.7 12.0 collective-permute-start
  693.6 13.4 collective-permute-start
  707.9 13.7 collective-permute-start
  722.6 12.0 collective-permute-start
  759.9 628.2 %all-reduce.7.cloned.1.call-start = ((), (), s32[]{:S(2)}) async-start(), calls=%async_computation.4 | async-start | bytes 5308416
Sparse Core Ops, SparseCore 0:
  11.8 150.6 all-gather.9
  165.7 164.9 all-gather.7
  333.9 165.5 all-gather.5
  760.0 97.3 all-reduce.4
  860.4 527.6 all-reduce.6
where the time goes:
time: 1400 us
  waiting for transfers between devices  1210 us (86%)
  matrix products  49.4 us (4%)
  local copies, waits for them, and re-layouts  40.1 us (3%)
  starting transfers between devices  33 us (2%)
  other arithmetic  22.9 us (2%)
  blocking collectives  22.1 us (2%)
  between operations  17.1 us (1%)
    unnamed x7, waiting for transfers between devices  621 us
    all_gather x1, waiting for transfers between devices, body(): lax.all_gather(narrowing_kernel, 'dp', axis=1, tiled=True)  166 us
    all_gather x1, waiting for transfers between devices, body(): lax.all_gather(widening_kernel, 'dp', axis=2, tiled=True)  162 us
    all_gather x1, waiting for transfers between devices, body(): text_row_block = lax.all_gather(caption_vectors, 'dp', axis=0, tiled=True)  145 us
    ppermute x15, waiting for transfers between devices, from_behind(): return lax.ppermute(value, axis, pairs)  117 us
    dot_general x8, matrix products, section_block(): jnp.dot(activated, w_down, preferred_element_type=jnp.float32)  45.6 us
    ppermute x15, starting transfers between devices, from_behind(): return lax.ppermute(value, axis, pairs)  32.8 us
  transfers between devices with their start and end apart: 20, of which 20 were waited for; matrix products, arithmetic and copies ran while one was open for 2% of the time, Pallas kernels for 0%

commit v1 on v0

--- a/solution.py
+++ b/solution.py
@@ -71,7 +71,9 @@
     shift_addend = score_shift[0]
     caption_vectors = unit_rows(caption_outputs)
     up_full, down_full = (
-        lax.all_gather(widening_kernel, "dp", axis=2, tiled=True),
+        jnp.concatenate(
+            lax.all_to_all(jnp.stack([widening_kernel] * lax.axis_size("dp")), "dp", 0, 0), axis=2
+        ),
         lax.all_gather(narrowing_kernel, "dp", axis=1, tiled=True),
     )
     up_full = up_full[0]

time: 1400 us -> 1330 us (0.950)
  waiting for transfers between devices: 1210 us -> 1140 us
  starting transfers between devices: 33 us -> 53 us
    all_gather x1 -> x0, waiting for transfers between devices: 162 us -> none  [body(): lax.all_gather(widening_kernel, 'dp', axis=2, tiled=True)]
    all_gather x1, waiting for transfers between devices: 145 us -> 203 us  [body(): text_row_block = lax.all_gather(caption_vectors, 'dp', axis=0, tiled=True)]
    all_gather x1, waiting for transfers between devices: 166 us -> 195 us  [body(): lax.all_gather(narrowing_kernel, 'dp', axis=1, tiled=True)]
    all_gather x1 -> x0, local copies, waits for them, and re-layouts: 22 us -> none  [body(): lax.all_gather(widening_kernel, 'dp', axis=2, tiled=True)]
    all_to_all x0 -> x1, starting transfers between devices: none -> 20.1 us  [body(): lax.all_to_all(jnp.stack([widening_kernel] * lax.axis_size('dp')), 'dp',...]
    unnamed x7 -> x6, waiting for transfers between devices: 621 us -> 621 us
  transfers between devices with their start and end apart: 20 -> 20, of which waited for: 20 -> 19; matrix products, arithmetic and copies ran while one was open for 2% -> 1% of each run, Pallas kernels for 0% -> 0%
where the time goes in v1:
time: 1330 us
  waiting for transfers between devices  1140 us (86%)
  starting transfers between devices  53 us (4%)
  matrix products  49.4 us (4%)
  local copies, waits for them, and re-layouts  34.7 us (3%)
  blocking collectives  22.1 us (2%)
  other arithmetic  19.8 us (1%)
  between operations  17.2 us (1%)
    unnamed x6, waiting for transfers between devices  621 us
    all_gather x1, waiting for transfers between devices, body(): text_row_block = lax.all_gather(caption_vectors, 'dp', axis=0, tiled=True)  203 us
    all_gather x1, waiting for transfers between devices, body(): lax.all_gather(narrowing_kernel, 'dp', axis=1, tiled=True)  195 us
    ppermute x15, waiting for transfers between devices, from_behind(): return lax.ppermute(value, axis, pairs)  117 us
    dot_general x8, matrix products, section_block(): jnp.dot(activated, w_down, preferred_element_type=jnp.float32)  45.6 us
    ppermute x15, starting transfers between devices, from_behind(): return lax.ppermute(value, axis, pairs)  32.8 us
  transfers between devices with their start and end apart: 20, of which 19 were waited for; matrix products, arithmetic and copies ran while one was open for 1% of the time, Pallas kernels for 0%

profile of v1, /device:TPU:1, one launch (start us, length us, event | category | flops | bytes accessed | tf_op | source)
XLA Modules:
  0.0 1333.4 jit_solution(2036762031767396735)
XLA Ops:
  11.0 20.1 %all-to-all-start = ((bf16[64,1,1152,34]{2,3,1,0:T(8,128)(2,1)}), bf16[64,1,1152,34]{2,3,1,0:T(8,128)(2,1)}, u32[]{:S(2)}, u32[]{:S(2)}) async-start(bf16[64,1,1152,34]{2,3,1,0:T(8,128)(2,1)} %stack.2), calls=%async_computation | async-start | bytes 11796480 | tf_op jit(solution)/shard_map/all_to_all | solution.py:75
  34.6 203.2 %all-gather.7.cloned.1.call-done = bf16[64,9,1152]{2,1,0:T(8,128)(2,1)} async-done(((bf16[1,9,1152]{2,1,0:T(8,128)(2,1)}), bf16[64,9,1152]{2,1,0:T(8,128)(2,1)}) %all-gather.7.cloned.1.call-update) | async-done | bytes 1327120 | tf_op jit(solution)/shard_map/all_gather | solution.py:105
  240.5 195.1 %all-gather.5.cloned.1.call-done = bf16[1,2176,1152]{2,0,1:T(2,128)(2,1)} async-done(((bf16[1,34,1152]{2,0,1:T(2,128)(2,1)}), bf16[1,2176,1152]{2,0,1:T(2,128)(2,1)}) %all-gather.5.cloned.1.call-update) | async-done | bytes 5013520 | tf_op jit(solution)/shard_map/all_gather | solution.py:77
  435.6 6.9 copy.18
  442.6 7.6 squeeze_reshape.3
  450.2 8.4 copy.15
  458.6 213.1 %while.14 = (s32[]{:T(128)}, bf16[64,1152]{1,0:T(8,128)(2,1)S(1)}, s32[]{:T(128)}, pred[]{:T(512)}, bf16[8,64,1152]{2,1,0:T(8,128)(2,1)}, /*index=5*/bf16[1152,2...) while((s32[]{:T(128)}, bf16[64,1152]{1,0:T(8,128)(2,1)S(1)}, ...), condition=%wide.region_5.6_spmd, body=%wide.region_0.5_spmd.sunk | while | flops 644014144 | bytes 11946512 | solution.py:96
  459.6 6.1 conditional.2
  467.6 7.3 collective-permute-done
  490.9 6.1 conditional.2
  505.9 6.1 conditional.2
  520.9 6.1 conditional.2
  535.9 6.1 conditional.2
  550.9 6.1 conditional.2
  565.9 6.1 conditional.2
  593.9 10.0 collective-permute-done
  606.9 10.0 collective-permute-done
  619.8 10.0 collective-permute-done
  632.7 11.4 collective-permute-done
  647.0 11.8 collective-permute-done
  661.7 10.1 collective-permute-done
  673.2 22.1 %all-gather = bf16[8,9,1152]{2,1,0:T(8,128)(2,1)S(1)} all-gather(bf16[1,9,1152]{2,1,0:T(8,128)(2,1)S(1)} %maximum_bitcast_fusion), channel_id=1, replica_groups=mesh['pipe'=8,'dp'=64] {'pipe'}, dimensions={0}, use_global_device_ids=true | all-gather | bytes 186624 | tf_op jit(solution)/shard_map/all_gather | solution.py:106
  703.0 91.5 %all-reduce.5.cloned.1.call-done = bf16[72,1152]{1,0:T(8,128)(2,1)} async-done(((bf16[72,1152]{1,0:T(8,128)(2,1)}), bf16[72,1152]{1,0:T(8,128)(2,1)}) %all-reduce.5.cloned.1.call-update) | async-done | bytes 165904
  796.0 529.3 %all-reduce.7.cloned.1.call-done = f32[576,1152]{1,0:T(8,128)} async-done(((f32[576,1152]{1,0:T(8,128)}), f32[576,1152]{1,0:T(8,128)}) %all-reduce.7.cloned.1.call-update) | async-done | bytes 2654224
  (138 shorter events, 166.7 us)
Async XLA Ops:
  10.9 20.2 %copy-start = (bf16[9,1152]{1,0:T(8,128)(2,1)S(1)}, bf16[9,1152]{1,0:T(8,128)(2,1)}, u32[]{:S(2)}) copy-start(bf16[9,1152]{1,0:T(8,128)(2,1)} %param.15) | copy-start | bytes 62212
  11.0 21.1 %copy-start.2 = (bf16[1,34,1152]{2,1,0:T(8,128)(2,1)S(1)}, bf16[1,34,1152]{2,1,0:T(8,128)(2,1)}, u32[]{:S(2)}) copy-start(bf16[1,34,1152]{2,1,0:T(8,128)(2,1)} %param.14) | copy-start | bytes 235012
  11.0 23.2 %copy-start.3 = (s32[4608]{0:T(1024)S(1)}, s32[4608]{0:T(1024)}, u32[]{:S(2)}) copy-start(s32[4608]{0:T(1024)} %param.17) | copy-start | bytes 55300
  11.0 23.5 %copy-start.1 = (f32[8,1152]{1,0:T(8,128)S(1)}, f32[8,1152]{1,0:T(8,128)}, u32[]{:S(2)}) copy-start(f32[8,1152]{1,0:T(8,128)} %param.16) | copy-start | bytes 110596
  11.0 431.6 %all-to-all-start = ((bf16[64,1,1152,34]{2,3,1,0:T(8,128)(2,1)}), bf16[64,1,1152,34]{2,3,1,0:T(8,128)(2,1)}, u32[]{:S(2)}, u32[]{:S(2)}) async-start(bf16[64,1,1152,34]{2,3,1,0:T(8,128)(2,1)} %stack.2), calls=%async_computation | async-start | bytes 11796480 | tf_op jit(solution)/shard_map/all_to_all | solution.py:75
  31.1 206.8 %all-gather.7.cloned.1.call-start = ((), (), s32[]{:S(2)}) async-start(), calls=%async_computation.2 | async-start | bytes 2396160 | tf_op jit(solution)/shard_map/all_gather | solution.py:105
  32.0 403.7 %all-gather.5.cloned.1.call-start = ((), (), s32[]{:S(2)}) async-start(), calls=%async_computation.1 | async-start | bytes 10183680 | tf_op jit(solution)/shard_map/all_gather | solution.py:77
  32.8 761.7 %all-reduce.5.cloned.1.call-start = ((), (), s32[]{:S(2)}) async-start(), calls=%async_computation.3 | async-start | bytes 331776
  465.7 9.2 collective-permute-start
  481.9 8.0 collective-permute-start
  496.9 8.0 collective-permute-start
  512.0 8.0 collective-permute-start
  527.0 8.0 collective-permute-start
  542.0 8.0 collective-permute-start
  557.0 8.0 collective-permute-start
  572.0 8.0 collective-permute-start
  581.0 10.1 collective-permute-start
  592.0 12.0 collective-permute-start
  604.9 12.0 collective-permute-start
  617.8 12.0 collective-permute-start
  630.8 13.4 %collective-permute-start = (bf16[64,1152]{1,0:T(8,128)(2,1)S(1)}, bf16[64,1152]{1,0:T(8,128)(2,1)S(1)}, u32[]{:S(2)}, u32[]{:S(2)}) collective-permute-start(bf16[64,1152]{1,0:T(8,128)(2,1)S(1)} %get-tuple-element.270), channel_id=1, source_target_pairs={{0,64},{64,128},{128,192},{192,256},{256,320},{320,384},{384,448},... | collective-permute-start | bytes 442376 | tf_op jit(solution)/shard_map/while/body/eval_jaxpr/ppermute | solution.py:10
  645.1 13.7 %collective-permute-start = (bf16[64,1152]{1,0:T(8,128)(2,1)S(1)}, bf16[64,1152]{1,0:T(8,128)(2,1)S(1)}, u32[]{:S(2)}, u32[]{:S(2)}) collective-permute-start(bf16[64,1152]{1,0:T(8,128)(2,1)S(1)} %get-tuple-element.270), channel_id=1, source_target_pairs={{0,64},{64,128},{128,192},{192,256},{256,320},{320,384},{384,448},... | collective-permute-start | bytes 442376 | tf_op jit(solution)/shard_map/while/body/eval_jaxpr/ppermute | solution.py:10
  659.7 12.0 collective-permute-start
  697.1 628.2 %all-reduce.7.cloned.1.call-start = ((), (), s32[]{:S(2)}) async-start(), calls=%async_computation.4 | async-start | bytes 5308416
Sparse Core Ops, SparseCore 0:
  35.7 202.1 all-gather.6
  241.0 194.5 all-gather.4
  697.2 97.2 all-reduce.4
  797.6 527.6 all-reduce.6
